TPU v7x, 128 devices: a whole 4x4x4 slice. The times are simulated.
128 devices in a mesh: seq: 32 (over x, z, core), head: 4 (over y).
Axes of the slice: x: 4, y: 4, z: 4, core: 2. Of those that a mesh axis runs over, the one named last changes fastest.
Arguments:
- tokens: bfloat16 [16384, 1024], P('seq'), may hold values from -6 to 6
- segment_ids: int32 [16384], replicated, may hold values from 0 to 4, as said below
- mix_gain: float32 [1024], replicated, may hold values from 0.1 to 1.9
- in_weight: bfloat16 [1024, 3, 1024], P(None, None, 'head'), may hold values from -0.1875 to 0.1875
- conv_weight: bfloat16 [3, 1024], P(None, 'head'), may hold values from -3 to 3
- out_weight: bfloat16 [1024, 1024], P(None, 'head'), may hold values from -0.1875 to 0.1875
- ffn_gain: float32 [1024], replicated, may hold values from 0.1 to 1.9
- gate_weight: bfloat16 [1024, 4608], P(None, 'head'), may hold values from -0.1875 to 0.1875
- up_weight: bfloat16 [1024, 4608], P(None, 'head'), may hold values from -0.1875 to 0.1875
- down_weight: bfloat16 [1024, 4608], P(None, 'head'), may hold values from -0.125 to 0.125
- cotangent: bfloat16 [16384, 1024], P('seq'), may hold values from -6 to 6
Outputs:
- result: bfloat16 [16384, 1024], P('seq')
- grad_tokens: float32 [16384, 1024], P('seq')
- grad_mix_gain: float32 [1024], replicated
- grad_in_weight: float32 [1024, 3, 1024], P('seq', None, 'head')
- grad_conv_weight: float32 [3, 1024], P(None, 'head')
- grad_out_weight: float32 [1024, 1024], P('seq', 'head')
- grad_ffn_gain: float32 [1024], replicated
- grad_gate_weight: float32 [1024, 4608], P('seq', 'head')
- grad_up_weight: float32 [1024, 4608], P('seq', 'head')
- grad_down_weight: float32 [1024, 4608], P('seq', 'head')
Inputs may be any that keep to these rules, and one draw needn't show every extreme that they name: `segment_ids`: ids start at 0, never fall along the tokens and rise by one at each sequence boundary; the tokens of one id form one sequence of at most 4096 tokens.
All inputs are finite; a program needn't handle non-finite values.
Results may differ from a plain program's by a relative error of at most 0.0095.
Values sent between devices are 32-bit elements; how exact they have to be, the bound alone decides.
A program may use at most 128 MiB of HBM per device.

v0:
```python
import jax
import jax.numpy as jnp
from jax import lax
from jax.sharding import PartitionSpec as P

EPS = 1e-05


def from_behind(block, axis, distance):
    devices = range(lax.axis_size(axis))
    route = [(i - distance, i) for i in devices if i - distance in devices]
    return lax.ppermute(block, axis, route)


def copy_for_each(x, axis):
    copies = jnp.broadcast_to(x, (lax.axis_size(axis), *x.shape))
    return lax.all_to_all(copies, axis, split_axis=0, concat_axis=0, tiled=True)


def of_everyone(x, axis):
    return copy_for_each(x, axis).sum(axis=0)


def in_one(arrays, axis):
    ends = [0]
    for a in arrays:
        ends.append(ends[-1] + a.size)
    so_far = of_everyone(jnp.concatenate([a.ravel() for a in arrays]), axis)
    return tuple((so_far[b:e].reshape(a.shape) for a, b, e in zip(arrays, ends, ends[1:])))


def in_one_piece(arrays, axis, dim, along):
    columns = [a.reshape(*a.shape[:along], -1) for a in arrays]
    both = jnp.concatenate(columns, axis=along)
    whole, at, finished = (lax.psum_scatter(both, axis, scatter_dimension=dim, tiled=True), 0, [])
    for a, column in zip(arrays, columns):
        piece = whole[..., at : at + column.shape[along]]
        finished.append(piece.reshape(*piece.shape[:along], *a.shape[along:]))
        at += column.shape[along]
    return tuple(finished)


def rms_scale(values):
    return lax.rsqrt(jnp.mean(values * values, axis=-1, keepdims=True) + EPS)


def norm_back(grad_normed, values, scale, gain):
    weighted = grad_normed * gain
    inner = jnp.mean(weighted * values, axis=-1, keepdims=True)
    grad_values = scale * weighted - values * (scale * scale * scale) * inner
    gain_grad = jnp.sum(grad_normed * values * scale, axis=0)
    return (grad_values, gain_grad)


def right_product(left, right):
    return lax.dot_general(
        left, right, (((1,), (1,)), ((), ())), preferred_element_type=jnp.float32
    )


def token_product(left, right):
    return lax.dot_general(
        left, right, (((0,), (0,)), ((), ())), preferred_element_type=jnp.float32
    )


def on_device(
    tokens,
    segment_ids,
    mix_gain,
    in_weight,
    conv_weight,
    out_weight,
    ffn_gain,
    gate_weight,
    up_weight,
    down_weight,
    cotangent,
):
    tok_rows = tokens.shape[0]
    first_row = lax.axis_index("seq") * tok_rows
    padded_ids = jnp.concatenate(
        [jnp.full((2,), -1, jnp.int32), segment_ids, jnp.full((2,), -2, jnp.int32)]
    )
    id_window = lax.dynamic_slice_in_dim(padded_ids, first_row, tok_rows + 4)
    near_ext = (id_window[2 : tok_rows + 4] == id_window[1 : tok_rows + 3]).astype(jnp.float32)
    far_ext = (id_window[2 : tok_rows + 4] == id_window[0 : tok_rows + 2]).astype(jnp.float32)
    near_own = near_ext[:tok_rows, None]
    far_own = far_ext[:tok_rows, None]
    inputs = tokens.astype(jnp.float32)
    mix_scale = rms_scale(inputs)
    mix_normed = (inputs * mix_scale * mix_gain).astype(jnp.bfloat16)
    projected = jnp.einsum("td,dkc->tkc", mix_normed, in_weight, preferred_element_type=jnp.float32)
    chan_b = projected[:, 0]
    chan_c = projected[:, 1]
    chan_x = projected[:, 2]
    mixed = chan_b * chan_x
    edge_rows = from_behind(mixed[tok_rows - 2 :], "seq", 1)
    extended = jnp.concatenate([edge_rows, mixed])
    kernel = conv_weight.astype(jnp.float32)
    prev_one = extended[1 : tok_rows + 1]
    prev_two = extended[0:tok_rows]
    conv_out = kernel[0] * mixed + kernel[1] * near_own * prev_one + kernel[2] * far_own * prev_two
    gated = (chan_c * conv_out).astype(jnp.bfloat16)
    resid = inputs + lax.psum(right_product(gated, out_weight), "head")
    ffn_scale = rms_scale(resid)
    ffn_normed = (resid * ffn_scale * ffn_gain).astype(jnp.bfloat16)
    gate = jnp.dot(ffn_normed, gate_weight, preferred_element_type=jnp.float32)
    upper = jnp.dot(ffn_normed, up_weight, preferred_element_type=jnp.float32)
    sigma = jax.nn.sigmoid(gate)
    act = (gate * sigma * upper).astype(jnp.bfloat16)
    result = (resid + lax.psum(right_product(act, down_weight), "head")).astype(jnp.bfloat16)
    d_act = jnp.dot(cotangent, down_weight, preferred_element_type=jnp.float32)
    d_gate = (d_act * upper * sigma * (1.0 + gate * (1.0 - sigma))).astype(jnp.bfloat16)
    d_up = (d_act * gate * sigma).astype(jnp.bfloat16)
    grad_down = token_product(cotangent, act)
    grad_gate = token_product(ffn_normed, d_gate)
    grad_up = token_product(ffn_normed, d_up)
    d_normed = lax.psum(right_product(d_gate, gate_weight) + right_product(d_up, up_weight), "head")
    d_hidden, grad_ffn_gain = norm_back(d_normed, resid, ffn_scale, ffn_gain)
    d_resid = d_hidden + cotangent.astype(jnp.float32)
    d_resid_low = d_resid.astype(jnp.bfloat16)
    d_gated = jnp.dot(d_resid_low, out_weight, preferred_element_type=jnp.float32)
    grad_out = token_product(d_resid_low, gated)
    d_chan_c = d_gated * conv_out
    d_conv = d_gated * chan_c
    tail_rows = from_behind(d_conv[:2], "seq", -1)
    later = jnp.concatenate([d_conv, tail_rows])
    d_mixed = (
        kernel[0] * d_conv
        + kernel[1] * near_ext[1 : tok_rows + 1, None] * later[1 : tok_rows + 1]
        + kernel[2] * far_ext[2 : tok_rows + 2, None] * later[2 : tok_rows + 2]
    )
    grad_conv = jnp.stack(
        [
            jnp.sum(d_conv * mixed, axis=0),
            jnp.sum(d_conv * near_own * prev_one, axis=0),
            jnp.sum(d_conv * far_own * prev_two, axis=0),
        ]
    )
    d_projected = jnp.stack([d_mixed * chan_x, d_chan_c, d_mixed * chan_b], axis=1).astype(
        jnp.bfloat16
    )
    grad_in = jnp.einsum("td,tkc->dkc", mix_normed, d_projected, preferred_element_type=jnp.float32)
    d_mix_normed = lax.psum(
        jnp.einsum("tkc,dkc->td", d_projected, in_weight, preferred_element_type=jnp.float32),
        "head",
    )
    d_inputs, grad_mix_gain = norm_back(d_mix_normed, inputs, mix_scale, mix_gain)
    grad_tokens = d_resid + d_inputs
    conv_total, gain_totals = in_one((grad_conv, jnp.stack([grad_mix_gain, grad_ffn_gain])), "seq")
    in_share, out_share, gate_share, up_share, down_share = in_one_piece(
        (grad_in, grad_out, grad_gate, grad_up, grad_down), "seq", 0, 1
    )
    return (
        result,
        grad_tokens,
        gain_totals[0],
        in_share,
        conv_total,
        out_share,
        gain_totals[1],
        gate_share,
        up_share,
        down_share,
    )


def solution(mesh):
    placed = (
        P("seq", None),
        P(),
        P(),
        P(None, None, "head"),
        P(None, "head"),
        P(None, "head"),
        P(),
        P(None, "head"),
        P(None, "head"),
        P(None, "head"),
        P("seq", None),
    )
    return jax.shard_map(
        on_device,
        mesh=mesh,
        in_specs=placed,
        out_specs=(
            P("seq", None),
            P("seq", None),
            P(),
            P("seq", None, "head"),
            P(None, "head"),
            P("seq", "head"),
            P(),
            P("seq", "head"),
            P("seq", "head"),
            P("seq", "head"),
        ),
        check_vma=False,
    )
```

profile of v0, /device:TPU:0, one launch (start us, length us, event | category | flops | bytes accessed | tf_op | source)
XLA Modules:
  0.0 405.6 jit_solution(4112243098430087586)
XLA Ops:
  7.2 1.7 fusion
  8.9 2.8 fusion.12
  11.7 1.2 copy-done.11
  13.0 0.1 fusion.24
  13.1 1.3 collective-permute-start
  14.4 0.1 concatenate.15
  14.5 0.1 dynamic_slice.3
  14.6 0.1 fusion.28
  14.7 0.1 fusion.36
  14.7 0.4 collective-permute-done
  15.2 2.2 multiply_convert_fusion.7
  17.3 0.7 copy-done.15
  18.1 2.9 fusion.39
  21.0 0.0 all-reduce.7.cloned.1.call-start
  21.1 64.1 %all-reduce.5.cloned.1.call-done = f32[512,1024]{1,0:T(8,128)} async-done(((f32[512,1024]{1,0:T(8,128)}), f32[512,1024]{1,0:T(8,128)}) %all-reduce.5.cloned.1.call-update) | async-done | bytes 2097168 | tf_op jit(solution)/shard_map/psum | solution.py:105
  85.1 1.9 multiply_reduce_fusion.2
  87.1 0.2 multiply_convert_fusion.3
  87.4 2.1 copy-done.32
  89.5 1.5 fusion.40
  91.1 0.5 copy-done.33
  91.6 1.5 fusion.41
  93.1 3.3 multiply_convert_fusion
  96.4 1.5 fusion.43
  98.0 2.9 convolution_add_fusion
  101.0 58.6 %all-reduce.7.cloned.1.call-done = f32[512,1024]{1,0:T(8,128)} async-done(((f32[512,1024]{1,0:T(8,128)}), f32[512,1024]{1,0:T(8,128)}) %all-reduce.7.cloned.1.call-update) | async-done | bytes 2097168 | tf_op jit(solution)/shard_map/psum | solution.py:119
  159.6 2.9 multiply_reduce_fusion
  162.5 0.5 copy-done.10
  163.0 1.9 convert_add_fusion.1
  165.0 0.4 fusion.21
  165.4 1.7 copy-done.12
  167.1 0.1 copy-done.14
  167.2 0.2 copy-done.18
  167.4 0.3 multiply_reduce_fusion.4
  167.7 1.5 collective-permute-start.1
  169.2 2.9 fusion.42
  172.1 0.3 fusion.25
  172.4 0.1 fusion.27
  172.5 1.0 copy-done.34
  173.5 2.4 convolution_bitcast_fusion
  176.0 0.0 reduce-scatter.2.cloned.1.call-start
  176.0 0.9 copy-done.27
  176.9 2.7 fusion.10
  179.6 3.6 copy.39
  183.2 4.3 %constant_dynamic-update-slice_fusion = f32[1024,4480]{1,0:T(8,128)} fusion(f32[1024,768]{1,0:T(8,128)} %copy.39), kind=kLoop, calls=%fused_computation.68 | loop fusion | bytes 6291456
  187.5 1.5 convolution_dynamic-update-slice_fusion.2
  189.0 0.4 copy-done.23
  189.4 4.0 convolution_dynamic-update-slice_fusion.1
  193.5 3.8 convolution_dynamic-update-slice_fusion
  197.3 3.9 bitcast_dynamic-update-slice_fusion
  201.2 68.6 %all-reduce.9.cloned.1.call-done = (f32[512,1024]{1,0:T(8,128)}, f32[512,1024]{1,0:T(8,128)}) async-done(((f32[512,1024]{1,0:T(8,128)}, f32[512,1024]{1,0:T(8,128)}), (f32[512,1024]{1,0:T(8,128)}, f32[512,1024]{1,0:T(8,128)})) %all-reduce.9.cloned.1.call-update) | async-done | bytes 4194320 | tf_op jit(solution)/shard_map/psum | solution.py:112
  269.8 2.3 fusion.8
  272.2 0.9 broadcast_in_dim.2
  273.1 7.3 %all-to-all-start = ((f32[32,1,2816]{2,1,0:T(1,128)}), f32[32,1,2816]{2,1,0:T(1,128)}, u32[]{:S(2)}, u32[]{:S(2)}) async-start(f32[32,1,2816]{2,1,0:T(1,128)} %broadcast_in_dim.2), calls=%async_computation | async-start | bytes 720896 | tf_op jit(solution)/shard_map/all_to_all | solution.py:17
  280.5 3.6 fusion.5
  284.1 1.3 add_convert_fusion
  285.4 4.7 %all-to-all-done = f32[32,1,2816]{2,1,0:T(1,128)} async-done(((f32[32,1,2816]{2,1,0:T(1,128)}), f32[32,1,2816]{2,1,0:T(1,128)}, u32[]{:S(2)}, u32[]{:S(2)}) %all-to-all-start) | async-done | bytes 360480 | tf_op jit(solution)/shard_map/all_to_all | solution.py:17
  290.1 1.2 reduce_sum.99
  291.4 0.6 slice.122
  292.0 0.6 fusion.35
  292.6 101.8 %reduce-scatter.2.cloned.1.call-done = f32[32,4480]{1,0:T(8,128)} async-done(((f32[1024,4480]{1,0:T(8,128)}), f32[32,4480]{1,0:T(8,128)}) %reduce-scatter.2.cloned.1.call-update) | async-done | bytes 573456 | tf_op jit(solution)/shard_map/reduce_scatter | solution.py:35
  394.3 0.9 slice.141
  395.2 0.6 copy.53
  395.9 1.8 fusion.34
  397.7 1.4 slice.143
  (85 shorter events, 0.4 us)
Async XLA Ops:
  7.2 85.9 %copy-start = (bf16[1024,1152]{1,0:T(8,128)(2,1)S(1)}, bf16[1024,1152]{1,0:T(8,128)(2,1)}, u32[]{:S(2)}) copy-start(bf16[1024,1152]{1,0:T(8,128)(2,1)} %param.20) | copy-start | bytes 7077892
  7.2 78.0 %all-reduce.5.cloned.1.call-start = ((), (), s32[]{:S(2)}) async-start(), calls=%async_computation.2 | async-start | bytes 4194304 | tf_op jit(solution)/shard_map/psum | solution.py:105
  8.9 5.5 %copy-start.28 = (s32[16384]{0:T(1024)S(1)}, s32[16384]{0:T(1024)}, u32[]{:S(2)}) copy-start(s32[16384]{0:T(1024)} %param.12) | copy-start | bytes 196612
  8.9 5.8 %copy-start.31 = (bf16[3,256]{1,0:T(4,128)(2,1)S(1)}, bf16[3,256]{1,0:T(4,128)(2,1)}, u32[]{:S(2)}) copy-start(bf16[3,256]{1,0:T(4,128)(2,1)} %param.15) | copy-start | bytes 4612
  11.7 1.2 copy-start.11
  13.0 4.3 %copy-start.13 = (f32[512,256]{1,0:T(8,128)}, f32[512,256]{1,0:T(8,128)S(1)}, u32[]{:S(2)}) copy-start(f32[512,256]{1,0:T(8,128)S(1)} %fusion.24) | copy-start | bytes 1572868
  13.1 2.1 collective-permute-start
  17.3 0.7 copy-start.15
  18.1 67.1 %copy-start.7 = (bf16[512,1024]{1,0:T(8,128)(2,1)S(1)}, bf16[512,1024]{1,0:T(8,128)(2,1)}, u32[]{:S(2)}) copy-start(bf16[512,1024]{1,0:T(8,128)(2,1)} %param.11) | copy-start | bytes 3145732
  21.0 66.1 %copy-start.29 = (f32[1024]{0:T(1024)S(1)}, f32[1024]{0:T(1024)}, u32[]{:S(2)}) copy-start(f32[1024]{0:T(1024)} %param.17) | copy-start | bytes 12292
  21.0 138.5 %all-reduce.7.cloned.1.call-start = ((), (), s32[]{:S(2)}) async-start(), calls=%async_computation.3 | async-start | bytes 4194304 | tf_op jit(solution)/shard_map/psum | solution.py:119
  87.1 4.0 copy-start.2
  87.1 2.4 copy-start.32
  89.5 1.6 copy-start.8
  89.5 2.0 copy-start.33
  91.6 1.6 copy-start.24
  96.4 1.6 copy-start.22
  96.4 1.6 copy-start.20
  100.9 168.9 %all-reduce.9.cloned.1.call-start = ((), (), s32[]{:S(2)}) async-start(), calls=%async_computation.5 | async-start | bytes 8388608 | tf_op jit(solution)/shard_map/psum | solution.py:112
  159.6 2.9 copy-start.3
  159.6 3.5 copy-start.10
  163.0 1.9 copy-start.19
  164.9 2.8 copy-start.5
  165.0 2.2 copy-start.12
  165.0 2.3 copy-start.14
  165.0 2.4 copy-start.18
  165.4 3.8 copy-start.35
  167.7 4.8 %copy-start.26 = (bf16[512,1,256]{2,0,1:T(8,128)(2,1)}, bf16[512,1,256]{2,0,1:T(8,128)(2,1)S(1)}, u32[]{:S(2)}) copy-start(bf16[512,1,256]{2,0,1:T(8,128)(2,1)S(1)} %get-tuple-element.72) | copy-start | bytes 786436
  167.7 4.4 %collective-permute-start.1 = (f32[2,256]{1,0:T(2,128)S(1)}, f32[2,256]{1,0:T(2,128)S(1)}, u32[]{:S(2)}, u32[]{:S(2)}) collective-permute-start(f32[2,256]{1,0:T(2,128)S(1)} %slice.137), channel_id=1, source_target_pairs={{4,0},{8,4},{12,8},{16,12},{20,16},{24,20},{28,24},{32,28},{36,32}... | collective-permute-start | bytes 6152 | tf_op jit(solution)/shard_map/ppermute | solution.py:12
  172.1 1.4 copy-start.34
  175.9 0.9 copy-start.27
  175.9 1.0 copy-start.30
  176.0 218.4 %reduce-scatter.2.cloned.1.call-start = ((), (), s32[]{:S(2)}) async-start(), calls=%async_computation.4 | async-start | bytes 18923520 | tf_op jit(solution)/shard_map/reduce_scatter | solution.py:35
  183.2 4.3 %copy-start.6 = (f32[512,1024]{1,0:T(8,128)S(1)}, f32[512,1024]{1,0:T(8,128)}, u32[]{:S(2)}) copy-start(f32[512,1024]{1,0:T(8,128)} %copy-done.5) | copy-start | bytes 6291460
  183.2 4.3 %copy-start.16 = (bf16[512,256]{1,0:T(8,128)(2,1)S(1)}, bf16[512,256]{1,0:T(8,128)(2,1)}, u32[]{:S(2)}) copy-start(bf16[512,256]{1,0:T(8,128)(2,1)} %copy-done.15) | copy-start | bytes 786436
  187.5 1.5 copy-start.9
  187.5 2.0 copy-start.23
  189.4 4.0 copy-start.21
  193.5 3.8 copy-start.25
  193.5 3.8 copy-start.36
  273.1 17.0 %all-to-all-start = ((f32[32,1,2816]{2,1,0:T(1,128)}), f32[32,1,2816]{2,1,0:T(1,128)}, u32[]{:S(2)}, u32[]{:S(2)}) async-start(f32[32,1,2816]{2,1,0:T(1,128)} %broadcast_in_dim.2), calls=%async_computation | async-start | bytes 720896 | tf_op jit(solution)/shard_map/all_to_all | solution.py:17
  280.5 3.6 copy-start.4
  280.5 3.6 copy-start.17
  284.1 115.0 %copy-start.1 = (bf16[1024,1152]{1,0:T(8,128)(2,1)S(1)}, bf16[1024,1152]{1,0:T(8,128)(2,1)}, u32[]{:S(2)}) copy-start(bf16[1024,1152]{1,0:T(8,128)(2,1)} %param.20) | copy-start | bytes 7077892
Sparse Core Ops, SparseCore 0:
  21.1 63.9 all-reduce.4
  101.0 58.4 all-reduce.6
  176.1 93.6 all-reduce.8
  274.2 120.0 reduce-scatter.1
where the time goes:
time: 406 us
  waiting for transfers between devices  298 us (73%)
  matrix products  38.2 us (9%)
  local copies, waits for them, and re-layouts  24.5 us (6%)
  other arithmetic  20.2 us (5%)
  between operations  14.2 us (3%)
  starting transfers between devices  10.3 us (3%)
    reduce_scatter x1, waiting for transfers between devices, in_one_piece(): lax.psum_scatter(both, axis, scatter_dimension=dim, tiled=True)  102 us
    psum x1, waiting for transfers between devices, on_device(): lax.psum(right_product(act, down_weight), 'head')  68.6 us
    psum x1, waiting for transfers between devices, on_device(): resid = inputs + lax.psum(right_product(gated, out_weight), 'head')  64.1 us
    psum x1, waiting for transfers between devices, on_device(): lax.psum(right_product(d_gate, gate_weight) + right_product(d_up, up_weig...  58.6 us
    unnamed x76, local copies, waits for them, and re-layouts  13.7 us
    dot_general x4, matrix products, token_product(): lax.dot_general(left, right, (((0,), (0,)), ((), ())), preferred_element_...  13.2 us
    dot_general x4, matrix products, right_product(): lax.dot_general(left, right, (((1,), (1,)), ((), ())), preferred_element_...  10.2 us
  transfers between devices with their start and end apart: 7, of which 6 were waited for; matrix products, arithmetic and copies ran while one was open for 9% of the time, Pallas kernels for 0%

commit v1 on v0

--- a/solution.py
+++ b/solution.py
@@ -116,7 +116,14 @@
     grad_down = token_product(cotangent, act)
     grad_gate = token_product(ffn_normed, d_gate)
     grad_up = token_product(ffn_normed, d_up)
-    d_normed = lax.psum(right_product(d_gate, gate_weight) + right_product(d_up, up_weight), "head")
+
+    def treat_the_vector(buf, named_axis):
+        t1 = jax.lax.all_gather(buf, axis_name=named_axis).sum(axis=0)
+        return t1
+
+    d_normed = treat_the_vector(
+        right_product(d_gate, gate_weight) + right_product(d_up, up_weight), "head"
+    )
     d_hidden, grad_ffn_gain = norm_back(d_normed, resid, ffn_scale, ffn_gain)
     d_resid = d_hidden + cotangent.astype(jnp.float32)
     d_resid_low = d_resid.astype(jnp.bfloat16)

time: 406 us -> 437 us (1.076)
  waiting for transfers between devices: 298 us -> 323 us
  other arithmetic: 20.2 us -> 26.4 us
    all_gather x0 -> x1, waiting for transfers between devices: none -> 82.9 us  [treat_the_vector(): t1 = jax.lax.all_gather(buf, axis_name=named_axis).sum(axis=0)]
    psum x1 -> x0, waiting for transfers between devices: 58.6 us -> none  [on_device(): lax.psum(right_product(d_gate, gate_weight) + right_product(d_up, up_weig...]
    reduce_sum x0 -> x1, other arithmetic: none -> 5.88 us  [treat_the_vector(): t1 = jax.lax.all_gather(buf, axis_name=named_axis).sum(axis=0)]
where the time goes in v1:
time: 437 us
  waiting for transfers between devices  323 us (74%)
  matrix products  38.2 us (9%)
  other arithmetic  26.4 us (6%)
  local copies, waits for them, and re-layouts  24 us (5%)
  between operations  14.2 us (3%)
  starting transfers between devices  10.5 us (2%)
    reduce_scatter x1, waiting for transfers between devices, in_one_piece(): lax.psum_scatter(both, axis, scatter_dimension=dim, tiled=True)  101 us
    all_gather x1, waiting for transfers between devices, treat_the_vector(): t1 = jax.lax.all_gather(buf, axis_name=named_axis).sum(axis=0)  82.9 us
    psum x1, waiting for transfers between devices, on_device(): lax.psum(right_product(act, down_weight), 'head')  70.2 us
    psum x1, waiting for transfers between devices, on_device(): resid = inputs + lax.psum(right_product(gated, out_weight), 'head')  64.1 us
    unnamed x76, local copies, waits for them, and re-layouts  13.3 us
    dot_general x4, matrix products, token_product(): lax.dot_general(left, right, (((0,), (0,)), ((), ())), preferred_element_...  13.2 us
    dot_general x4, matrix products, right_product(): lax.dot_general(left, right, (((1,), (1,)), ((), ())), preferred_element_...  10.2 us
  transfers between devices with their start and end apart: 7, of which 6 were waited for; matrix products, arithmetic and copies ran while one was open for 9% of the time, Pallas kernels for 0%

profile of v1, /device:TPU:0, one launch (start us, length us, event | category | flops | bytes accessed | tf_op | source)
XLA Modules:
  0.0 436.6 jit_solution(3690214051269826683)
XLA Ops:
  7.2 1.7 fusion
  8.9 2.8 fusion.12
  11.7 1.2 copy-done.11
  13.1 1.3 collective-permute-start
  14.4 0.1 concatenate.15
  14.5 0.1 dynamic_slice.3
  14.6 0.1 fusion.28
  14.7 0.1 fusion.36
  14.7 0.4 collective-permute-done
  15.2 2.2 multiply_convert_fusion.7
  17.3 0.7 copy-done.15
  18.1 2.9 fusion.39
  21.1 64.1 %all-reduce.4.cloned.1.call-done = f32[512,1024]{1,0:T(8,128)} async-done(((f32[512,1024]{1,0:T(8,128)}), f32[512,1024]{1,0:T(8,128)}) %all-reduce.4.cloned.1.call-update) | async-done | bytes 2097168 | tf_op jit(solution)/shard_map/psum | solution.py:105
  85.1 1.9 multiply_reduce_fusion.2
  87.1 0.2 multiply_convert_fusion.3
  87.4 2.1 copy-done.32
  89.5 1.5 fusion.40
  91.1 0.5 copy-done.33
  91.6 1.5 fusion.41
  93.1 3.3 multiply_convert_fusion
  96.4 1.5 fusion.43
  98.0 2.9 convolution_add_fusion
  100.9 0.2 all-reduce.6.cloned.1.call-start
  101.1 82.9 %all-gather.3.cloned.1.call-done = f32[2048,1024]{1,0:T(8,128)} async-done(((f32[512,1024]{1,0:T(8,128)}), f32[2048,1024]{1,0:T(8,128)}) %all-gather.3.cloned.1.call-update) | async-done | bytes 8388624 | tf_op jit(solution)/shard_map/all_gather | solution.py:121
  184.0 5.9 %reduce_sum.101 = f32[512,1024]{1,0:T(8,128)} reduce(f32[4,512,1024]{2,1,0:T(8,128)} %bitcast.80, f32[]{:T(128)} %constant.6.clone.1), dimensions={0}, to_apply=%region_4.0 | reduce | flops 1572864 | bytes 10485764 | tf_op jit(solution)/shard_map/reduce_sum | solution.py:121
  189.9 2.9 multiply_reduce_fusion
  192.8 0.5 copy-done.7
  193.4 1.9 convert_add_fusion.1
  195.3 0.4 fusion.21
  195.8 1.7 copy-done.12
  197.5 0.1 copy-done.14
  197.6 0.2 copy-done.18
  197.7 0.3 multiply_reduce_fusion.4
  198.1 1.3 collective-permute-start.1
  199.4 2.9 fusion.42
  202.3 0.3 fusion.25
  202.6 0.1 fusion.27
  202.7 1.0 copy-done.34
  203.7 2.4 convolution_bitcast_fusion
  206.1 0.3 reduce-scatter.2.cloned.1.call-start
  206.4 0.7 copy-done.27
  207.1 2.7 fusion.10
  209.8 3.6 copy.39
  213.4 4.0 constant_dynamic-update-slice_fusion
  217.4 1.5 convolution_dynamic-update-slice_fusion.2
  218.9 0.4 copy-done.23
  219.4 4.0 convolution_dynamic-update-slice_fusion.1
  223.4 3.8 convolution_dynamic-update-slice_fusion
  227.2 3.9 bitcast_dynamic-update-slice_fusion
  231.1 70.2 %all-reduce.6.cloned.1.call-done = (f32[512,1024]{1,0:T(8,128)}, f32[512,1024]{1,0:T(8,128)}) async-done(((f32[512,1024]{1,0:T(8,128)}, f32[512,1024]{1,0:T(8,128)}), (f32[512,1024]{1,0:T(8,128)}, f32[512,1024]{1,0:T(8,128)})) %all-reduce.6.cloned.1.call-update) | async-done | bytes 4194320 | tf_op jit(solution)/shard_map/psum | solution.py:112
  301.3 2.3 fusion.8
  303.7 0.9 broadcast_in_dim.2
  304.6 7.3 %all-to-all-start = ((f32[32,1,2816]{2,1,0:T(1,128)}), f32[32,1,2816]{2,1,0:T(1,128)}, u32[]{:S(2)}, u32[]{:S(2)}) async-start(f32[32,1,2816]{2,1,0:T(1,128)} %broadcast_in_dim.2), calls=%async_computation | async-start | bytes 720896 | tf_op jit(solution)/shard_map/all_to_all | solution.py:17
  312.0 4.0 fusion.5
  316.0 1.3 add_convert_fusion
  317.3 4.4 all-to-all-done
  321.6 1.2 reduce_sum.109
  322.9 0.6 slice.122
  323.5 0.6 fusion.35
  324.1 101.2 %reduce-scatter.2.cloned.1.call-done = f32[32,4480]{1,0:T(8,128)} async-done(((f32[1024,4480]{1,0:T(8,128)}), f32[32,4480]{1,0:T(8,128)}) %reduce-scatter.2.cloned.1.call-update) | async-done | bytes 573456 | tf_op jit(solution)/shard_map/reduce_scatter | solution.py:35
  425.3 0.9 slice.141
  426.2 0.6 copy.53
  426.8 1.8 fusion.34
  428.7 1.4 slice.143
  (86 shorter events, 0.4 us)
Async XLA Ops:
  7.2 85.9 %copy-start = (bf16[1024,1152]{1,0:T(8,128)(2,1)S(1)}, bf16[1024,1152]{1,0:T(8,128)(2,1)}, u32[]{:S(2)}) copy-start(bf16[1024,1152]{1,0:T(8,128)(2,1)} %param.20) | copy-start | bytes 7077892
  7.2 78.0 %all-reduce.4.cloned.1.call-start = ((), (), s32[]{:S(2)}) async-start(), calls=%async_computation.2 | async-start | bytes 4194304 | tf_op jit(solution)/shard_map/psum | solution.py:105
  8.9 5.5 %copy-start.28 = (s32[16384]{0:T(1024)S(1)}, s32[16384]{0:T(1024)}, u32[]{:S(2)}) copy-start(s32[16384]{0:T(1024)} %param.12) | copy-start | bytes 196612
  8.9 5.8 %copy-start.31 = (bf16[3,256]{1,0:T(4,128)(2,1)S(1)}, bf16[3,256]{1,0:T(4,128)(2,1)}, u32[]{:S(2)}) copy-start(bf16[3,256]{1,0:T(4,128)(2,1)} %param.15) | copy-start | bytes 4612
  11.7 1.2 copy-start.11
  13.0 4.3 copy-start.13
  13.1 2.1 collective-permute-start
  17.3 0.7 copy-start.15
  18.1 67.1 %copy-start.8 = (bf16[512,1024]{1,0:T(8,128)(2,1)S(1)}, bf16[512,1024]{1,0:T(8,128)(2,1)}, u32[]{:S(2)}) copy-start(bf16[512,1024]{1,0:T(8,128)(2,1)} %param.11) | copy-start | bytes 3145732
  21.0 66.1 %copy-start.29 = (f32[1024]{0:T(1024)S(1)}, f32[1024]{0:T(1024)}, u32[]{:S(2)}) copy-start(f32[1024]{0:T(1024)} %param.17) | copy-start | bytes 12292
  21.0 163.0 %all-gather.3.cloned.1.call-start = ((), (), s32[]{:S(2)}) async-start(), calls=%async_computation.4 | async-start | bytes 10485760 | tf_op jit(solution)/shard_map/all_gather | solution.py:121
  87.1 4.0 copy-start.2
  87.1 2.4 copy-start.32
  89.5 1.6 copy-start.9
  89.5 2.0 copy-start.33
  91.6 1.6 copy-start.24
  96.4 1.6 copy-start.22
  96.4 1.6 copy-start.20
  100.9 200.4 %all-reduce.6.cloned.1.call-start = ((), (), s32[]{:S(2)}) async-start(), calls=%async_computation.5 | async-start | bytes 8388608 | tf_op jit(solution)/shard_map/psum | solution.py:112
  189.9 2.9 copy-start.3
  189.9 3.5 copy-start.7
  193.4 1.9 copy-start.19
  195.3 2.8 copy-start.5
  195.3 2.2 copy-start.12
  195.3 2.3 copy-start.14
  195.3 2.4 copy-start.18
  195.8 3.6 copy-start.35
  198.1 4.6 %copy-start.26 = (bf16[512,1,256]{2,0,1:T(8,128)(2,1)}, bf16[512,1,256]{2,0,1:T(8,128)(2,1)S(1)}, u32[]{:S(2)}) copy-start(bf16[512,1,256]{2,0,1:T(8,128)(2,1)S(1)} %get-tuple-element.72) | copy-start | bytes 786436
  198.1 4.2 collective-permute-start.1
  202.3 1.4 copy-start.34
  206.1 0.9 copy-start.27
  206.1 1.0 copy-start.30
  206.1 219.2 %reduce-scatter.2.cloned.1.call-start = ((), (), s32[]{:S(2)}) async-start(), calls=%async_computation.3 | async-start | bytes 18923520 | tf_op jit(solution)/shard_map/reduce_scatter | solution.py:35
  213.4 4.0 copy-start.6
  213.4 4.0 copy-start.16
  217.4 1.5 copy-start.10
  217.4 2.0 copy-start.23
  219.4 4.0 copy-start.21
  223.4 3.8 copy-start.25
  223.4 3.8 copy-start.36
  304.6 17.0 %all-to-all-start = ((f32[32,1,2816]{2,1,0:T(1,128)}), f32[32,1,2816]{2,1,0:T(1,128)}, u32[]{:S(2)}, u32[]{:S(2)}) async-start(f32[32,1,2816]{2,1,0:T(1,128)} %broadcast_in_dim.2), calls=%async_computation | async-start | bytes 720896 | tf_op jit(solution)/shard_map/all_to_all | solution.py:17
  312.0 4.0 copy-start.4
  312.0 4.0 copy-start.17
  316.0 114.1 %copy-start.1 = (bf16[1024,1152]{1,0:T(8,128)(2,1)S(1)}, bf16[1024,1152]{1,0:T(8,128)(2,1)}, u32[]{:S(2)}) copy-start(bf16[1024,1152]{1,0:T(8,128)(2,1)} %param.20) | copy-start | bytes 7077892
Sparse Core Ops, SparseCore 0:
  21.1 63.9 all-reduce.3
  101.0 82.9 all-gather.2
  206.3 95.0 all-reduce.5
  305.2 120.0 reduce-scatter.1
